TPU v7x, 256 devices: a whole 4x4x8 slice. The times are simulated.
256 devices in a mesh: dp: 4 (over y_lo, core), tm: 4 (over x), rows: 16 (over z, y_hi).
Axes of the slice: x: 4, y: 4 (y_hi: 2, y_lo: 2; y = y_hi * 2 + y_lo), z: 8, core: 2. Of those that a mesh axis runs over, the one named last changes fastest.
Arguments:
- latents: bfloat16 [4, 8, 16, 30, 512], P('dp', 'tm', 'rows'), may hold values from -6 to 6
- grad_out: bfloat16 [4, 8, 32, 60, 256], P('dp', 'tm', 'rows'), may hold values from -6 to 6
- kernel: bfloat16 [3, 3, 3, 512, 256], replicated, may hold values from -0.0546875 to 0.0546875
Outputs:
- grad_latents: bfloat16 [4, 8, 16, 30, 512], P('dp', 'tm', 'rows')
- weight_grad: float32 [512, 3, 3, 3, 256], P(('dp', 'tm', 'rows'))
All inputs are finite; a program needn't handle non-finite values.
Results may differ from a plain program's by a relative error of at most 0.001.
Values may be sent and summed in bfloat16 or wider, within the bound.
A program may use at most 128 MiB of HBM per device.

v0:
```python
import jax
import jax.numpy as jnp
from jax import lax
from jax.sharding import PartitionSpec as P


def shift_from(shard, axis, by):
    peers = lax.axis_size(axis)
    pairs = [(i, i + by) for i in range(peers) if 0 <= i + by < peers]
    return lax.ppermute(shard, axis, pairs)


def pool_pairs(values, dim):
    n = values.shape[dim] // 2
    pad = [(0, 0)] * values.ndim
    pad[dim] = (1, 1)
    ext = jnp.pad(values, pad)
    shape = values.shape
    shifted = ext.reshape(shape[:dim] + (n + 1, 2) + shape[dim + 1 :]).sum(axis=dim + 1)
    aligned = values.reshape(shape[:dim] + (n, 2) + shape[dim + 1 :]).sum(axis=dim + 1)
    out = [
        lax.slice_in_dim(shifted, 1, n + 1, axis=dim),
        aligned,
        lax.slice_in_dim(shifted, 0, n, axis=dim),
    ]
    return jnp.stack(out, axis=dim + 1)


def with_halo(block, axis, dim, width):
    count = lax.axis_size(axis)
    forward = [(i, i + 1) for i in range(count - 1)]
    backward = [(target, source) for source, target in forward]
    low = lax.ppermute(
        lax.slice_in_dim(block, block.shape[dim] - width, None, axis=dim), axis, forward
    )
    high = lax.ppermute(lax.slice_in_dim(block, 0, width, axis=dim), axis, backward)
    return jnp.concatenate([low, block, high], axis=dim)


def body(latents, grad_out, kernel):
    frames = grad_out.shape[1]
    height = grad_out.shape[2]
    width = grad_out.shape[3]
    channels = latents.shape[4]
    outputs = grad_out.shape[4]
    devices = lax.axis_size("dp") * lax.axis_size("tm") * lax.axis_size("rows")
    factor = float(devices * frames * height * width) ** (-0.5)
    slab_count = lax.axis_size("rows")
    grad_whole = lax.all_gather(grad_out[0], "rows", axis=1, tiled=True)
    whole_height = grad_whole.shape[1]
    near = with_halo(grad_out[0], "rows", 1, 1)
    later = shift_from(near, "tm", -1)
    grad_all = jnp.concatenate([near, later], axis=0)
    grad_all = jnp.pad(grad_all, ((0, 0), (0, 0), (1, 1), (0, 0)))
    patches = []
    for a in range(3):
        for i in range(3):
            for j in range(3):
                patches.append(
                    grad_all[2 - a : 2 - a + frames, 2 - i : 2 - i + height, 2 - j : 2 - j + width]
                )
    patches = jnp.stack(patches, axis=3).reshape(frames * height * width, 27, outputs)
    grad_up = lax.dot_general(
        patches,
        kernel.reshape(27, channels, outputs),
        (((1, 2), (0, 2)), ((), ())),
        preferred_element_type=jnp.float32,
    )
    pooled = grad_up.reshape(frames, height // 2, 2, width // 2, 2, channels).sum(axis=(2, 4))
    grad_latents = pooled.astype(jnp.bfloat16)[None]
    groups = lax.axis_size("dp") * lax.axis_size("tm")
    share = channels // devices
    earlier = shift_from(latents, "tm", 1)
    with_earlier = jnp.concatenate([earlier, latents], axis=1)
    lead = with_earlier.shape[:4]
    regrouped = with_earlier.reshape(lead + (groups, slab_count, share))
    regrouped = jnp.swapaxes(regrouped, 4, 5).reshape(lead + (channels,))
    owned = lax.all_to_all(regrouped, "rows", split_axis=4, concat_axis=2, tiled=True)[0]
    group_channels = owned.shape[3]
    taps_a = jnp.stack([owned[a : a + frames] for a in range(3)], axis=0)
    pooled_grad = pool_pairs(pool_pairs(grad_whole.astype(jnp.float32), 1), 3)
    scaled = pooled_grad * 65537.0
    top = scaled - (scaled - pooled_grad)
    both = jnp.stack([top, pooled_grad - top], axis=0).astype(jnp.bfloat16)
    term = jnp.einsum("afrsc,xfrisjo->caijxo", taps_a, both, preferred_element_type=jnp.float32)
    term = (term[..., 0, :] + term[..., 1, :]) * factor
    term = term.reshape(group_channels, 3, 3, 3, outputs)
    term = lax.psum_scatter(term, "dp", scatter_dimension=0, tiled=True)
    weight_grad = lax.psum_scatter(term, "tm", scatter_dimension=0, tiled=True)
    return (grad_latents, weight_grad)


def solution(mesh):
    in_specs = (P("dp", "tm", "rows", None, None), P("dp", "tm", "rows", None, None), P())
    out_specs = (P("dp", "tm", "rows", None, None), P(("dp", "tm", "rows"), None, None, None, None))
    return jax.shard_map(body, mesh=mesh, in_specs=in_specs, out_specs=out_specs, check_vma=False)
```

profile of v0, /device:TPU:8, one launch (start us, length us, event | category | flops | bytes accessed | tf_op | source)
XLA Modules:
  0.0 247.5 jit_solution(9366353959574920145)
XLA Ops:
  7.2 3.4 %collective-permute-start.3 = (bf16[1,2,1,30,512]{4,1,3,2,0:T(2,128)(2,1)}, bf16[1,2,1,30,512]{4,1,3,2,0:T(2,128)(2,1)S(1)}, u32[]{:S(2)}, u32[]{:S(2)}) collective-permute-start(bf16[1,2,1,30,512]{4,1,3,2,0:T(2,128)(2,1)} %param.3), channel_id=1, source_target_pairs={{0,16},{16,32},{32,48},{1,17},{17,33},{33,49},{2,18},{18,34},{34,5... | collective-permute-start | bytes 184328 | tf_op jit(solution)/shard_map/ppermute | solution.py:10
  10.6 1.2 fusion.25
  11.8 4.2 %collective-permute-start = (bf16[2,1,60,256]{3,1,2,0:T(2,128)(2,1)S(1)}, bf16[2,1,60,256]{3,1,2,0:T(2,128)(2,1)S(1)}, u32[]{:S(2)}, u32[]{:S(2)}) collective-permute-start(bf16[2,1,60,256]{3,1,2,0:T(2,128)(2,1)S(1)} %get-tuple-element.46), channel_id=1, source_target_pairs={{0,1},{1,2},{2,3},{3,4},{4,5},{5,6},{6,7},{7,8},{8,9},{9,10},{10,1... | collective-permute-start | bytes 184328 | tf_op jit(solution)/shard_map/ppermute | solution.py:33
  16.0 1.3 collective-permute-start.1
  17.3 1.6 copy.102
  19.0 1.3 dynamic-slice
  20.9 1.0 pad_maximum_fusion.5
  23.0 1.6 reshape.353
  24.7 12.5 %all-to-all-start = ((bf16[16,2,1920]{2,1,0:T(2,128)(2,1)}), bf16[16,2,1920]{2,1,0:T(2,128)(2,1)S(1)}, u32[]{:S(2)}, u32[]{:S(2)}) async-start(bf16[16,2,1920]{2,1,0:T(2,128)(2,1)} %reshape.353), calls=%async_computation | async-start | bytes 245760 | tf_op jit(solution)/shard_map/all_to_all | solution.py:78
  37.7 1.7 collective-permute-start.2
  39.9 8.4 %all-to-all-done = bf16[16,2,1920]{2,1,0:T(2,128)(2,1)S(1)} async-done(((bf16[16,2,1920]{2,1,0:T(2,128)(2,1)}), bf16[16,2,1920]{2,1,0:T(2,128)(2,1)S(1)}, u32[]{:S(2)}, u32[]{:S(2)}) %all-to-all-start) | async-done | bytes 122912 | tf_op jit(solution)/shard_map/all_to_all | solution.py:78
  48.4 1.4 reshape.354
  49.8 0.9 slice_bitcast_fusion.2
  51.4 0.7 pad_slice_fusion
  52.1 0.7 copy_dynamic-update-slice_fusion.26
  54.4 0.7 copy_dynamic-update-slice_fusion.23
  55.8 0.7 copy_dynamic-update-slice_fusion.21
  59.2 1.6 pad_slice_fusion.1
  61.5 0.7 copy_dynamic-update-slice_fusion.15
  62.8 0.7 copy_dynamic-update-slice_fusion.13
  64.2 0.7 copy_dynamic-update-slice_fusion.11
  64.9 0.7 copy_dynamic-update-slice_fusion.10
  66.3 0.7 copy_dynamic-update-slice_fusion.8
  66.9 41.3 %all-gather.3.cloned.1.call-done = bf16[1,2,32,60,256]{4,1,3,0,2:T(2,128)(2,1)} async-done(((bf16[1,2,2,60,256]{4,1,3,0,2:T(2,128)(2,1)}), bf16[1,2,32,60,256]{4,1,3,0,2:T(2,128)(2,1)}) %all-gather.3.cloned.1.call-update) | async-done | bytes 1966096 | tf_op jit(solution)/shard_map/all_gather | solution.py:49
  108.2 2.9 %convert_bitcast_fusion = f32[2,32,60,256]{3,0,2,1:T(2,128)S(1)} fusion(bf16[1,2,32,60,256]{4,1,3,0,2:T(2,128)(2,1)} %all-gather.3.cloned.1.call-done), kind=kLoop, calls=%fused_computation.21 | loop fusion | flops 983040 | bytes 5898240 | tf_op jit(solution)/shard_map/convert_element_type | solution.py:81
  111.1 3.4 %pad.13 = f32[2,34,60,256]{3,0,2,1:T(2,128)} pad(f32[2,32,60,256]{3,0,2,1:T(2,128)S(1)} %convert_bitcast_fusion, f32[]{:T(128)} %constant.3.clone.1), padding=0_0x1_1x0_0x0_0 | pad | bytes 8110084 | tf_op jit(solution)/shard_map/jit(_pad)/pad | solution.py:17
  114.5 5.3 %reduce_sum.46 = f32[2,17,60,256]{3,0,2,1:T(2,128)S(1)} reduce(f32[2,17,2,60,256]{4,0,3,2,1:T(2,128)} %bitcast.115, f32[]{:T(128)} %constant.3.clone.1), dimensions={2}, to_apply=%region_1.2 | reduce | flops 522240 | bytes 6266884 | tf_op jit(solution)/shard_map/reduce_sum | solution.py:19
  119.8 16.3 %fusion.23 = (f32[2,16,60,256]{3,0,2,1:T(2,128)}, f32[2,16,1,60,256]{4,0,3,1,2:T(2,128)}, f32[2,16,1,60,256]{4,0,3,1,2:T(2,128)}, f32[2,16,60,256]{3,0,2,1:T(2,128)}) fusion(f32[2,17,60,256]{3,0,2,1:T(2,128)S(1)} %reduce_sum.46), kind=kLoop, calls=%fused_computation.89 | loop fusion | bytes 11796480 | tf_op jit(solution)/shard_map/slice | solution.py:22
  136.1 4.7 %reduce_sum.47 = f32[2,16,60,256]{3,0,2,1:T(2,128)S(1)} reduce(bf16[2,16,2,60,256]{4,0,3,2,1:T(2,128)(2,1)} %bitcast.117, f32[]{:T(128)} %constant.3.clone.1), dimensions={2}, to_apply=%region_2.3 | reduce | flops 491520 | bytes 3932164 | tf_op jit(solution)/shard_map/reduce_sum | solution.py:20
  140.9 1.9 copy.106
  142.7 1.0 copy-done.4
  143.7 5.5 %select_maximum_fusion = f32[2,16,3,62,256]{4,0,3,1,2:T(2,128)} fusion(f32[2,16,1,60,256]{4,0,3,1,2:T(2,128)S(1)} %copy-done.4, f32[2,16,1,60,256]{4,0,3,1,2:T(2,128)S(1)} %bitcast.114, f32[2,16,1,60,256]{4,0,3,1,2:T(2,128)S(1)} %copy-done.3), kind=kLoop, calls=%fused_computation.10 | loop fusion | flops 12189696 | bytes 11993088 | tf_op jit(solution)/shard_map/stack | solution.py:26
  149.2 7.7 %reduce.2 = f32[2,16,3,31,256]{4,0,3,1,2:T(2,128)S(1)} reduce(f32[2,16,3,31,2,256]{5,0,4,3,1,2:T(2,128)} %bitcast.113, f32[]{:T(128)} %constant.3.clone.1), dimensions={4}, to_apply=%region_3.4 | reduce | flops 761856 | bytes 9142276
  156.9 1.5 fusion.22
  159.1 0.9 copy-done
  160.7 0.9 maximum_reduce_fusion
  161.5 1.7 copy.159
  163.2 1.0 copy_bitcast_fusion
  164.2 2.2 fusion.1
  166.5 1.7 fusion.8
  168.3 1.1 fusion.16
  171.5 0.7 copy_dynamic-update-slice_fusion.4
  172.2 0.7 copy_dynamic-update-slice_fusion.3
  174.9 12.6 %reduce-scatter.3.cloned.1.call-done = f32[8,3,3,3,256]{4,0,1,3,2:T(8,128)} async-done(((f32[32,3,3,3,256]{4,0,1,3,2:T(8,128)}), f32[8,3,3,3,256]{4,0,1,3,2:T(8,128)}) %reduce-scatter.3.cloned.1.call-update) | async-done | bytes 221200 | tf_op jit(solution)/shard_map/reduce_scatter | solution.py:88
  187.6 6.1 %fusion.12 = bf16[2,30,512]{2,1,0:T(8,128)(2,1)S(1)} fusion(bf16[27,512,256,1,1,1]{2,1,0,5,4,3:T(8,128)(2,1)} %bitcast.158, bf16[2,1,2,30,2,27,256]{6,3,5,4,2,0,1:T(8,128)(2,1)} %copy_dynamic-update-slice_fusion), kind=kOutput, calls=%fused_computation.20 | convolution fusion | flops 1698785280 | bytes 10457088 | tf_op jit(solution)/shard_map/dot_general | solution.py:63
  193.7 0.7 copy.114
  194.4 44.7 %all-reduce.6.cloned.1.call-done = f32[8,3,3,3,256]{4,0,1,3,2:T(8,128)} async-done(((f32[8,3,3,3,256]{4,0,1,3,2:T(8,128)}), f32[8,3,3,3,256]{4,0,1,3,2:T(8,128)}) %all-reduce.6.cloned.1.call-update) | async-done | bytes 221200
  239.1 1.0 constant_dynamic-slice_fusion
  (63 shorter events, 16.6 us)
Async XLA Ops:
  7.2 30.1 %copy-start.5 = (bf16[1,2,2,60,256]{4,2,3,1,0:T(2,128)(2,1)S(1)}, bf16[1,2,2,60,256]{4,2,3,1,0:T(2,128)(2,1)}, u32[]{:S(2)}) copy-start(bf16[1,2,2,60,256]{4,2,3,1,0:T(2,128)(2,1)} %param.4) | copy-start | bytes 368644
  7.2 101.0 %all-gather.3.cloned.1.call-start = ((), (), s32[]{:S(2)}) async-start(), calls=%async_computation.3 | async-start | bytes 2088960 | tf_op jit(solution)/shard_map/all_gather | solution.py:49
  7.2 13.7 %collective-permute-start.3 = (bf16[1,2,1,30,512]{4,1,3,2,0:T(2,128)(2,1)}, bf16[1,2,1,30,512]{4,1,3,2,0:T(2,128)(2,1)S(1)}, u32[]{:S(2)}, u32[]{:S(2)}) collective-permute-start(bf16[1,2,1,30,512]{4,1,3,2,0:T(2,128)(2,1)} %param.3), channel_id=1, source_target_pairs={{0,16},{16,32},{32,48},{1,17},{17,33},{33,49},{2,18},{18,34},{34,5... | collective-permute-start | bytes 184328 | tf_op jit(solution)/shard_map/ppermute | solution.py:10
  11.8 25.4 %collective-permute-start = (bf16[2,1,60,256]{3,1,2,0:T(2,128)(2,1)S(1)}, bf16[2,1,60,256]{3,1,2,0:T(2,128)(2,1)S(1)}, u32[]{:S(2)}, u32[]{:S(2)}) collective-permute-start(bf16[2,1,60,256]{3,1,2,0:T(2,128)(2,1)S(1)} %get-tuple-element.46), channel_id=1, source_target_pairs={{0,1},{1,2},{2,3},{3,4},{4,5},{5,6},{6,7},{7,8},{8,9},{9,10},{10,1... | collective-permute-start | bytes 184328 | tf_op jit(solution)/shard_map/ppermute | solution.py:33
  16.0 21.2 %collective-permute-start.1 = (bf16[2,1,60,256]{3,1,2,0:T(2,128)(2,1)S(1)}, bf16[2,1,60,256]{3,1,2,0:T(2,128)(2,1)S(1)}, u32[]{:S(2)}, u32[]{:S(2)}) collective-permute-start(bf16[2,1,60,256]{3,1,2,0:T(2,128)(2,1)S(1)} %get-tuple-element.47), channel_id=1, source_target_pairs={{1,0},{2,1},{3,2},{4,3},{5,4},{6,5},{7,6},{8,7},{9,8},{10,9},{11,1... | collective-permute-start | bytes 184328 | tf_op jit(solution)/shard_map/ppermute | solution.py:36
  24.7 23.7 %all-to-all-start = ((bf16[16,2,1920]{2,1,0:T(2,128)(2,1)}), bf16[16,2,1920]{2,1,0:T(2,128)(2,1)S(1)}, u32[]{:S(2)}, u32[]{:S(2)}) async-start(bf16[16,2,1920]{2,1,0:T(2,128)(2,1)} %reshape.353), calls=%async_computation | async-start | bytes 245760 | tf_op jit(solution)/shard_map/all_to_all | solution.py:78
  37.2 150.3 %reduce-scatter.3.cloned.1.call-start = ((), (), s32[]{:S(2)}) async-start(), calls=%async_computation.2 | async-start | bytes 1105920 | tf_op jit(solution)/shard_map/reduce_scatter | solution.py:88
  37.7 13.0 %collective-permute-start.2 = (bf16[2,4,60,256]{3,1,2,0:T(4,128)(2,1)S(1)}, bf16[2,4,60,256]{3,1,2,0:T(4,128)(2,1)S(1)}, u32[]{:S(2)}, u32[]{:S(2)}) collective-permute-start(bf16[2,4,60,256]{3,1,2,0:T(4,128)(2,1)S(1)} %pad_maximum_fusion.2), channel_id=1, source_target_pairs={{16,0},{32,16},{48,32},{17,1},{33,17},{49,33},{18,2},{34,18},{50,3... | collective-permute-start | bytes 737288 | tf_op jit(solution)/shard_map/ppermute | solution.py:10
  140.8 1.9 copy-start.3
  140.8 2.8 %copy-start.4 = (f32[2,16,1,60,256]{4,0,3,1,2:T(2,128)S(1)}, f32[2,16,1,60,256]{4,0,3,1,2:T(2,128)}, u32[]{:S(2)}) copy-start(f32[2,16,1,60,256]{4,0,3,1,2:T(2,128)} %get-tuple-element.16) | copy-start | bytes 5898244
  156.9 1.6 copy-start.1
  158.5 1.5 copy-start
  158.5 2.2 copy-start.2
  164.2 2.3 copy-start.10
  164.2 2.3 copy-start.11
  164.2 2.3 copy-start.12
  168.2 1.9 copy-start.9
  168.2 2.5 %copy-start.8 = (bf16[2,2,60,256]{3,1,2,0:T(2,128)(2,1)S(1)}, bf16[2,2,60,256]{3,1,2,0:T(2,128)(2,1)}, u32[]{:S(2)}) copy-start(bf16[2,2,60,256]{3,1,2,0:T(2,128)(2,1)} %get-tuple-element.37) | copy-start | bytes 368644
  168.2 3.9 %copy-start.7 = (bf16[2,2,60,256]{3,1,2,0:T(2,128)(2,1)S(1)}, bf16[2,2,60,256]{3,1,2,0:T(2,128)(2,1)}, u32[]{:S(2)}) copy-start(bf16[2,2,60,256]{3,1,2,0:T(2,128)(2,1)} %get-tuple-element.38) | copy-start | bytes 368644
  168.3 4.6 %copy-start.6 = (bf16[2,2,60,256]{3,1,2,0:T(2,128)(2,1)S(1)}, bf16[2,2,60,256]{3,1,2,0:T(2,128)(2,1)}, u32[]{:S(2)}) copy-start(bf16[2,2,60,256]{3,1,2,0:T(2,128)(2,1)} %get-tuple-element.31) | copy-start | bytes 368644
  169.4 69.7 %all-reduce.6.cloned.1.call-start = ((), (), s32[]{:S(2)}) async-start(), calls=%async_computation.4 | async-start | bytes 442368
Sparse Core Ops, SparseCore 0:
  19.1 89.0 all-gather.2
  169.5 17.9 reduce-scatter.2
  189.9 49.1 all-reduce.5
where the time goes:
time: 251 us; the launch traced here: 247 us
  waiting for transfers between devices  107 us (43%)
  local copies, waits for them, and re-layouts  61.5 us (25%)
  other arithmetic  32.8 us (13%)
  starting transfers between devices  23.2 us (9%)
  between operations  15 us (6%)
  matrix products  7.87 us (3%)
    unnamed x4, waiting for transfers between devices  44.8 us
    all_gather x1, waiting for transfers between devices, body(): grad_whole = lax.all_gather(grad_out[0], 'rows', axis=1, tiled=True)  41.3 us
    unnamed x59, local copies, waits for them, and re-layouts  27.8 us
    slice x3, local copies, waits for them, and re-layouts, pool_pairs(): lax.slice_in_dim(shifted, 1, n + 1, axis=dim)  18.5 us
    reduce_scatter x1, waiting for transfers between devices, body(): term = lax.psum_scatter(term, 'dp', scatter_dimension=0, tiled=True)  12.6 us
    all_to_all x1, starting transfers between devices, body(): lax.all_to_all(regrouped, 'rows', split_axis=4, concat_axis=2, tiled=True)  12.5 us
    all_to_all x1, waiting for transfers between devices, body(): lax.all_to_all(regrouped, 'rows', split_axis=4, concat_axis=2, tiled=True)  8.43 us
    unnamed x1, other arithmetic  7.74 us
  transfers between devices with their start and end apart: 8, of which 4 were waited for; matrix products, arithmetic and copies ran while one was open for 16% of the time, Pallas kernels for 0%

commit v1 on v0

--- a/solution.py
+++ b/solution.py
@@ -46,7 +46,9 @@
     devices = lax.axis_size("dp") * lax.axis_size("tm") * lax.axis_size("rows")
     factor = float(devices * frames * height * width) ** (-0.5)
     slab_count = lax.axis_size("rows")
-    grad_whole = lax.all_gather(grad_out[0], "rows", axis=1, tiled=True)
+    grad_whole = jnp.concatenate(
+        lax.all_to_all(jnp.stack([grad_out[0]] * lax.axis_size("rows")), "rows", 0, 0), axis=1
+    )
     whole_height = grad_whole.shape[1]
     near = with_halo(grad_out[0], "rows", 1, 1)
     later = shift_from(near, "tm", -1)

time: 251 us -> 214 us (0.85); the launches traced: 247 us -> 214 us
  local copies, waits for them, and re-layouts: 61.5 us -> 46.5 us
  waiting for transfers between devices: 107 us -> 92.3 us
  other arithmetic: 32.8 us -> 25.1 us
  starting transfers between devices: 23.2 us -> 26.8 us
    all_gather x1 -> x0, waiting for transfers between devices: 41.3 us -> none  [body(): grad_whole = lax.all_gather(grad_out[0], 'rows', axis=1, tiled=True)]
    all_to_all x0 -> x1, waiting for transfers between devices: none -> 28.6 us  [body(): lax.all_to_all(jnp.stack([grad_out[0]] * lax.axis_size('rows')), 'rows',...]
    slice x3, local copies, waits for them, and re-layouts: 18.5 us -> 5.57 us  [pool_pairs(): lax.slice_in_dim(shifted, 1, n + 1, axis=dim)]
    all_to_all x0 -> x1, starting transfers between devices: none -> 3.72 us  [body(): lax.all_to_all(jnp.stack([grad_out[0]] * lax.axis_size('rows')), 'rows',...]
    convert_element_type x1 -> x0, other arithmetic: 2.89 us -> none  [body(): pooled_grad = pool_pairs(pool_pairs(grad_whole.astype(jnp.float32), 1), 3)]
    reduce_sum x1, other arithmetic: 5.32 us -> 2.51 us  [pool_pairs(): ext.reshape(shape[:dim] + (n + 1, 2) + shape[dim + 1:]).sum(axis=dim + 1)]
    unnamed x59 -> x56, local copies, waits for them, and re-layouts: 27.8 us -> 25.2 us
    unnamed x4 -> x3, waiting for transfers between devices: 44.8 us -> 44.8 us
  transfers between devices with their start and end apart: 8 -> 8, of which waited for: 4 -> 4; matrix products, arithmetic and copies ran while one was open for 16% -> 20% of each run, Pallas kernels for 0% -> 0%
where the time goes in v1:
time: 214 us
  waiting for transfers between devices  92.3 us (43%)
  local copies, waits for them, and re-layouts  46.5 us (22%)
  starting transfers between devices  26.8 us (13%)
  other arithmetic  25.1 us (12%)
  between operations  15.1 us (7%)
  matrix products  7.87 us (4%)
    unnamed x3, waiting for transfers between devices  44.8 us
    all_to_all x1, waiting for transfers between devices, body(): lax.all_to_all(jnp.stack([grad_out[0]] * lax.axis_size('rows')), 'rows',...  28.6 us
    unnamed x56, local copies, waits for them, and re-layouts  25.2 us
    all_to_all x1, starting transfers between devices, body(): lax.all_to_all(regrouped, 'rows', split_axis=4, concat_axis=2, tiled=True)  12.5 us
    reduce_scatter x1, waiting for transfers between devices, body(): term = lax.psum_scatter(term, 'dp', scatter_dimension=0, tiled=True)  10.8 us
    all_to_all x1, waiting for transfers between devices, body(): lax.all_to_all(regrouped, 'rows', split_axis=4, concat_axis=2, tiled=True)  8.1 us
    unnamed x1, other arithmetic  7.74 us
    dot_general x1, matrix products, body(): lax.dot_general(patches, kernel.reshape(27, channels, outputs), (((1, 2),...  6.12 us
  transfers between devices with their start and end apart: 8, of which 4 were waited for; matrix products, arithmetic and copies ran while one was open for 20% of the time, Pallas kernels for 0%

profile of v1, /device:TPU:8, one launch (start us, length us, event | category | flops | bytes accessed | tf_op | source)
XLA Modules:
  0.0 213.7 jit_solution(15756712796282381123)
XLA Ops:
  7.2 3.5 %collective-permute-start.3 = (bf16[1,2,1,30,512]{4,1,3,2,0:T(2,128)(2,1)}, bf16[1,2,1,30,512]{4,1,3,2,0:T(2,128)(2,1)S(1)}, u32[]{:S(2)}, u32[]{:S(2)}) collective-permute-start(bf16[1,2,1,30,512]{4,1,3,2,0:T(2,128)(2,1)} %param.3), channel_id=1, source_target_pairs={{0,16},{16,32},{32,48},{1,17},{17,33},{33,49},{2,18},{18,34},{34,5... | collective-permute-start | bytes 184328 | tf_op jit(solution)/shard_map/ppermute | solution.py:10
  10.7 1.2 fusion.25
  11.9 4.2 %collective-permute-start = (bf16[2,1,60,256]{3,1,2,0:T(2,128)(2,1)S(1)}, bf16[2,1,60,256]{3,1,2,0:T(2,128)(2,1)S(1)}, u32[]{:S(2)}, u32[]{:S(2)}) collective-permute-start(bf16[2,1,60,256]{3,1,2,0:T(2,128)(2,1)S(1)} %get-tuple-element.46), channel_id=1, source_target_pairs={{0,1},{1,2},{2,3},{3,4},{4,5},{5,6},{6,7},{7,8},{8,9},{9,10},{10,1... | collective-permute-start | bytes 184328 | tf_op jit(solution)/shard_map/ppermute | solution.py:33
  16.1 1.3 collective-permute-start.1
  17.4 1.0 copy.103
  18.4 1.3 dynamic-slice
  20.4 1.0 pad_maximum_fusion.5
  22.5 1.7 reshape.358
  24.1 12.5 %all-to-all-start.1 = ((bf16[16,2,1920]{2,1,0:T(2,128)(2,1)}), bf16[16,2,1920]{2,1,0:T(2,128)(2,1)S(1)}, u32[]{:S(2)}, u32[]{:S(2)}) async-start(bf16[16,2,1920]{2,1,0:T(2,128)(2,1)} %reshape.358), calls=%async_computation.1 | async-start | bytes 245760 | tf_op jit(solution)/shard_map/all_to_all | solution.py:80
  36.7 1.1 pad_maximum_fusion.2
  37.8 1.3 collective-permute-start.2
  39.6 8.1 %all-to-all-done.1 = bf16[16,2,1920]{2,1,0:T(2,128)(2,1)S(1)} async-done(((bf16[16,2,1920]{2,1,0:T(2,128)(2,1)}), bf16[16,2,1920]{2,1,0:T(2,128)(2,1)S(1)}, u32[]{:S(2)}, u32[]{:S(2)}) %all-to-all-start.1) | async-done | bytes 122912 | tf_op jit(solution)/shard_map/all_to_all | solution.py:80
  47.7 2.3 %stack.165 = bf16[16,2,2,60,256]{4,1,3,2,0:T(2,128)(2,1)} broadcast(bf16[2,2,60,256]{3,0,2,1:T(2,128)(2,1)S(1)} %copy.103), dimensions={1,2,3,4} | broadcast | bytes 2088960 | tf_op jit(solution)/shard_map/stack | solution.py:50
  50.1 3.7 %all-to-all-start = ((bf16[16,2,2,60,256]{4,1,3,2,0:T(2,128)(2,1)}), bf16[16,2,2,60,256]{4,1,3,2,0:T(2,128)(2,1)S(1)}, u32[]{:S(2)}, u32[]{:S(2)}) async-start(bf16[16,2,2,60,256]{4,1,3,2,0:T(2,128)(2,1)} %stack.165), calls=%async_computation | async-start | bytes 3932160 | tf_op jit(solution)/shard_map/all_to_all | solution.py:50
  54.0 1.4 reshape.359
  55.5 0.9 slice_bitcast_fusion.2
  57.1 0.7 pad_slice_fusion
  59.4 0.7 copy_dynamic-update-slice_fusion.24
  61.4 0.7 copy_dynamic-update-slice_fusion.21
  62.8 0.7 copy_dynamic-update-slice_fusion.19
  64.8 1.6 pad_slice_fusion.1
  68.5 0.7 copy_dynamic-update-slice_fusion.13
  69.8 0.7 copy_dynamic-update-slice_fusion.11
  71.2 0.7 copy_dynamic-update-slice_fusion.9
  71.9 0.7 copy_dynamic-update-slice_fusion.8
  72.6 28.6 %all-to-all-done = bf16[16,2,2,60,256]{4,1,3,2,0:T(2,128)(2,1)S(1)} async-done(((bf16[16,2,2,60,256]{4,1,3,2,0:T(2,128)(2,1)}), bf16[16,2,2,60,256]{4,1,3,2,0:T(2,128)(2,1)S(1)}, u32[]{:S(2)}, u32[]{:S(2)}) %all-to-all-start) | async-done | bytes 1966112 | tf_op jit(solution)/shard_map/all_to_all | solution.py:50
  101.2 1.6 pad.14
  102.8 2.5 %convert_reduce_fusion = f32[2,17,60,256]{3,0,2,1:T(2,128)S(1)} fusion(bf16[2,17,2,60,256]{4,0,3,2,1:T(2,128)(2,1)S(1)} %bitcast.120), kind=kLoop, calls=%fused_computation.13 | loop fusion | flops 1566720 | bytes 4177920 | tf_op jit(solution)/shard_map/reduce_sum | solution.py:19
  105.3 3.4 %fusion.23 = (f32[2,16,60,256]{3,0,2,1:T(2,128)}, f32[2,16,1,60,256]{4,0,3,1,2:T(2,128)S(1)}, f32[2,16,1,60,256]{4,0,3,1,2:T(2,128)S(1)}, f32[2,16,60,256]{3,0,2,1:T(2,128)}) fusion(f32[2,17,60,256]{3,0,2,1:T(2,128)S(1)} %convert_reduce_fusion), kind=kLoop, calls=%fused_computation.90 | loop fusion | bytes 11796480 | tf_op jit(solution)/shard_map/slice | solution.py:22
  108.7 2.4 %convert_reduce_fusion.1 = f32[16,2,60,256]{3,1,2,0:T(2,128)S(1)} fusion(bf16[16,2,2,60,256]{4,1,3,2,0:T(2,128)(2,1)S(1)} %all-to-all-done), kind=kLoop, calls=%fused_computation.14 | loop fusion | flops 1474560 | bytes 3932160 | tf_op jit(solution)/shard_map/reduce_sum | solution.py:20
  111.1 5.5 %select_maximum_fusion = f32[2,16,3,62,256]{4,0,3,1,2:T(2,128)} fusion(f32[2,16,1,60,256]{4,0,3,1,2:T(2,128)S(1)} %get-tuple-element.16, f32[2,16,1,60,256]{4,0,3,1,2:T(2,128)S(1)} %bitcast.117, f32[2,16,1,60,256]{4,0,3,1,2:T(2,128)S(1)} %get-tuple-element.15), kind=kLoop, calls=%fused_computation.10 | loop fusion | flops 12189696 | bytes 11993088 | tf_op jit(solution)/shard_map/stack | solution.py:26
  116.6 7.7 %reduce.3 = f32[2,16,3,31,256]{4,0,3,1,2:T(2,128)S(1)} reduce(f32[2,16,3,31,2,256]{5,0,4,3,1,2:T(2,128)} %bitcast.115, f32[]{:T(128)} %constant.8.clone.1), dimensions={4}, to_apply=%region_3.4 | reduce | flops 761856 | bytes 9142276
  124.4 1.5 fusion.22
  126.6 0.9 copy-done.2
  128.8 0.8 maximum_reduce_fusion
  129.6 1.7 copy.160
  131.3 1.2 copy_bitcast_fusion
  132.5 1.9 fusion.1
  134.5 1.8 fusion.8
  136.3 1.1 fusion.16
  138.1 0.7 copy_dynamic-update-slice_fusion.6
  140.8 0.7 copy_dynamic-update-slice_fusion.2
  141.5 0.7 copy_dynamic-update-slice_fusion.1
  142.9 10.8 %reduce-scatter.3.cloned.1.call-done = f32[8,3,3,3,256]{4,0,1,3,2:T(8,128)} async-done(((f32[32,3,3,3,256]{4,0,1,3,2:T(8,128)}), f32[8,3,3,3,256]{4,0,1,3,2:T(8,128)}) %reduce-scatter.3.cloned.1.call-update) | async-done | bytes 221200 | tf_op jit(solution)/shard_map/reduce_scatter | solution.py:90
  153.7 6.1 %fusion.12 = bf16[2,30,512]{2,1,0:T(8,128)(2,1)S(1)} fusion(bf16[27,512,256,1,1,1]{2,1,0,5,4,3:T(8,128)(2,1)} %bitcast.162, bf16[2,1,2,30,2,27,256]{6,3,5,4,2,0,1:T(8,128)(2,1)} %copy_dynamic-update-slice_fusion), kind=kOutput, calls=%fused_computation.22 | convolution fusion | flops 1698785280 | bytes 10457088 | tf_op jit(solution)/shard_map/dot_general | solution.py:65
  159.9 0.7 copy.115
  160.6 44.7 %all-reduce.6.cloned.1.call-done = f32[8,3,3,3,256]{4,0,1,3,2:T(8,128)} async-done(((f32[8,3,3,3,256]{4,0,1,3,2:T(8,128)}), f32[8,3,3,3,256]{4,0,1,3,2:T(8,128)}) %all-reduce.6.cloned.1.call-update) | async-done | bytes 221200
  205.3 1.0 constant_dynamic-slice_fusion
  (60 shorter events, 17.0 us)
Async XLA Ops:
  7.2 29.5 %copy-start.4 = (bf16[1,2,2,60,256]{4,2,3,1,0:T(2,128)(2,1)S(1)}, bf16[1,2,2,60,256]{4,2,3,1,0:T(2,128)(2,1)}, u32[]{:S(2)}) copy-start(bf16[1,2,2,60,256]{4,2,3,1,0:T(2,128)(2,1)} %param.4) | copy-start | bytes 368644
  7.2 13.2 %collective-permute-start.3 = (bf16[1,2,1,30,512]{4,1,3,2,0:T(2,128)(2,1)}, bf16[1,2,1,30,512]{4,1,3,2,0:T(2,128)(2,1)S(1)}, u32[]{:S(2)}, u32[]{:S(2)}) collective-permute-start(bf16[1,2,1,30,512]{4,1,3,2,0:T(2,128)(2,1)} %param.3), channel_id=1, source_target_pairs={{0,16},{16,32},{32,48},{1,17},{17,33},{33,49},{2,18},{18,34},{34,5... | collective-permute-start | bytes 184328 | tf_op jit(solution)/shard_map/ppermute | solution.py:10
  11.9 24.8 %collective-permute-start = (bf16[2,1,60,256]{3,1,2,0:T(2,128)(2,1)S(1)}, bf16[2,1,60,256]{3,1,2,0:T(2,128)(2,1)S(1)}, u32[]{:S(2)}, u32[]{:S(2)}) collective-permute-start(bf16[2,1,60,256]{3,1,2,0:T(2,128)(2,1)S(1)} %get-tuple-element.46), channel_id=1, source_target_pairs={{0,1},{1,2},{2,3},{3,4},{4,5},{5,6},{6,7},{7,8},{8,9},{9,10},{10,1... | collective-permute-start | bytes 184328 | tf_op jit(solution)/shard_map/ppermute | solution.py:33
  16.1 20.6 %collective-permute-start.1 = (bf16[2,1,60,256]{3,1,2,0:T(2,128)(2,1)S(1)}, bf16[2,1,60,256]{3,1,2,0:T(2,128)(2,1)S(1)}, u32[]{:S(2)}, u32[]{:S(2)}) collective-permute-start(bf16[2,1,60,256]{3,1,2,0:T(2,128)(2,1)S(1)} %get-tuple-element.47), channel_id=1, source_target_pairs={{1,0},{2,1},{3,2},{4,3},{5,4},{6,5},{7,6},{8,7},{9,8},{10,9},{11,1... | collective-permute-start | bytes 184328 | tf_op jit(solution)/shard_map/ppermute | solution.py:36
  24.1 23.6 %all-to-all-start.1 = ((bf16[16,2,1920]{2,1,0:T(2,128)(2,1)}), bf16[16,2,1920]{2,1,0:T(2,128)(2,1)S(1)}, u32[]{:S(2)}, u32[]{:S(2)}) async-start(bf16[16,2,1920]{2,1,0:T(2,128)(2,1)} %reshape.358), calls=%async_computation.1 | async-start | bytes 245760 | tf_op jit(solution)/shard_map/all_to_all | solution.py:80
  37.8 18.6 %collective-permute-start.2 = (bf16[2,4,60,256]{3,1,2,0:T(4,128)(2,1)}, bf16[2,4,60,256]{3,1,2,0:T(4,128)(2,1)S(1)}, u32[]{:S(2)}, u32[]{:S(2)}) collective-permute-start(bf16[2,4,60,256]{3,1,2,0:T(4,128)(2,1)} %pad_maximum_fusion.2), channel_id=1, source_target_pairs={{16,0},{32,16},{48,32},{17,1},{33,17},{49,33},{18,2},{34,18},{50,3... | collective-permute-start | bytes 737288 | tf_op jit(solution)/shard_map/ppermute | solution.py:10
  50.1 51.1 %all-to-all-start = ((bf16[16,2,2,60,256]{4,1,3,2,0:T(2,128)(2,1)}), bf16[16,2,2,60,256]{4,1,3,2,0:T(2,128)(2,1)S(1)}, u32[]{:S(2)}, u32[]{:S(2)}) async-start(bf16[16,2,2,60,256]{4,1,3,2,0:T(2,128)(2,1)} %stack.165), calls=%async_computation | async-start | bytes 3932160 | tf_op jit(solution)/shard_map/all_to_all | solution.py:50
  53.8 99.9 %reduce-scatter.3.cloned.1.call-start = ((), (), s32[]{:S(2)}) async-start(), calls=%async_computation.3 | async-start | bytes 1105920 | tf_op jit(solution)/shard_map/reduce_scatter | solution.py:90
  111.1 5.5 %copy-start = (f32[16,2,60,256]{3,1,2,0:T(2,128)}, f32[16,2,60,256]{3,1,2,0:T(2,128)S(1)}, u32[]{:S(2)}) copy-start(f32[16,2,60,256]{3,1,2,0:T(2,128)S(1)} %convert_reduce_fusion.1) | copy-start | bytes 5898244
  124.4 1.6 copy-start.3
  125.9 1.5 copy-start.2
  125.9 2.2 %copy-start.1 = (f32[16,2,60,256]{3,1,2,0:T(2,128)S(1)}, f32[16,2,60,256]{3,1,2,0:T(2,128)}, u32[]{:S(2)}) copy-start(f32[16,2,60,256]{3,1,2,0:T(2,128)} %copy-done) | copy-start | bytes 5898244
  132.5 1.9 copy-start.9
  132.5 1.9 copy-start.10
  132.5 1.9 copy-start.11
  136.2 1.9 copy-start.8
  136.2 2.5 %copy-start.7 = (bf16[2,2,60,256]{3,1,2,0:T(2,128)(2,1)S(1)}, bf16[2,2,60,256]{3,1,2,0:T(2,128)(2,1)}, u32[]{:S(2)}) copy-start(bf16[2,2,60,256]{3,1,2,0:T(2,128)(2,1)} %get-tuple-element.37) | copy-start | bytes 368644
  136.2 3.9 %copy-start.6 = (bf16[2,2,60,256]{3,1,2,0:T(2,128)(2,1)S(1)}, bf16[2,2,60,256]{3,1,2,0:T(2,128)(2,1)}, u32[]{:S(2)}) copy-start(bf16[2,2,60,256]{3,1,2,0:T(2,128)(2,1)} %get-tuple-element.38) | copy-start | bytes 368644
  136.2 4.6 %copy-start.5 = (bf16[2,2,60,256]{3,1,2,0:T(2,128)(2,1)S(1)}, bf16[2,2,60,256]{3,1,2,0:T(2,128)(2,1)}, u32[]{:S(2)}) copy-start(bf16[2,2,60,256]{3,1,2,0:T(2,128)(2,1)} %get-tuple-element.31) | copy-start | bytes 368644
  137.4 67.9 %all-reduce.6.cloned.1.call-start = ((), (), s32[]{:S(2)}) async-start(), calls=%async_computation.4 | async-start | bytes 442368
Sparse Core Ops, SparseCore 0:
  137.5 16.1 reduce-scatter.2
  156.1 49.1 all-reduce.5
